TPU v7x, 128 devices: a whole 4x4x4 slice. The times are simulated.
128 devices in a mesh: occ: 4 (over x), vir: 32 (over y, z, core).
Axes of the slice: x: 4, y: 4, z: 4, core: 2. Of those that a mesh axis runs over, the one named last changes fastest.
Arguments:
- amplitudes: bfloat16 [256, 262144], P('occ', 'vir'), may hold values from -6 to 6
- cycle_integrals: bfloat16 [16, 64, 16, 64], P(None, None, 'occ'), may hold values from -0.1875 to 0.1875
- ladder_tiles: bfloat16 [2048, 4, 128, 128], P('vir'), may hold values from -0.25 to 0.25
- ladder_rows: int32 [2048, 4], P('vir'), may hold values from 0 to 2047, as said below
- ladder_count: int32 [2048], P('vir'), may hold values from 2 to 4
- row_gap: float32 [256], P('occ'), may hold values from 1 to 3
- column_energy: float32 [262144], P('vir'), may hold values from 0.5 to 8
Outputs:
- updated: bfloat16 [256, 262144], P('occ', 'vir')
Inputs may be any that keep to these rules, and one draw needn't show every extreme that they name: `ladder_rows`: each entry of column tile c's list names a virtual-pair tile within 2 tiles of c; entry 0 is max(c - 2, 0) and entry 1 is min(c + 2, 2047).
All inputs are finite; a program needn't handle non-finite values.
Results may differ from a plain program's by a relative error of at most 0.0019.
Values may be sent and summed in bfloat16 or wider, within the bound.
A program may use at most 192 MiB of HBM per device.

v0:
```python
import jax
import jax.numpy as jnp
from jax import lax
from jax.sharding import PartitionSpec as P

TILE = 128
NJ = 16
NA = 4096
NB_DEV = 2
KMAX = 4
HT = 2


def extended(block, sides, width):
    for axis, dim in sides:
        count = lax.axis_size(axis)
        forward = [(i, i + 1) for i in range(count - 1)]
        backward = [(target, source) for source, target in forward]
        low = lax.ppermute(
            lax.slice_in_dim(block, block.shape[dim] - width, None, axis=dim), axis, forward
        )
        high = lax.ppermute(lax.slice_in_dim(block, 0, width, axis=dim), axis, backward)
        block = jnp.concatenate([low, block, high], axis=dim)
    return block


def local(
    amplitudes, cycle_integrals, ladder_tiles, ladder_rows, ladder_count, row_gap, column_energy
):
    rows_dev = amplitudes.shape[0]
    cols_dev = amplitudes.shape[1]
    outer_occ = rows_dev // NJ
    four_dim = amplitudes.reshape(outer_occ, NJ, NB_DEV, NA)
    cycle_input = lax.all_to_all(four_dim, "vir", split_axis=3, concat_axis=2, tiled=True)
    tiles_dev = cols_dev // TILE
    padded = extended(amplitudes, (("vir", 1),), HT * TILE)
    own_tiles = lax.axis_index("vir") * tiles_dev + jnp.arange(tiles_dev, dtype=jnp.int32)
    relative = ladder_rows - own_tiles[:, None]
    live_mask = jnp.arange(KMAX, dtype=jnp.int32)[None, :] < ladder_count[:, None]
    ladder = jnp.zeros((rows_dev, tiles_dev, TILE), jnp.float32)
    for offset in range(2 * HT + 1):
        window = padded[:, offset * TILE : offset * TILE + cols_dev].reshape(
            rows_dev, tiles_dev, TILE
        )
        for entry in range(KMAX):
            selected = live_mask[:, entry] & (relative[:, entry] == offset - HT)
            masked = jnp.where(
                selected[:, None, None], ladder_tiles[:, entry], jnp.zeros((), jnp.bfloat16)
            )
            ladder = ladder + jnp.einsum(
                "rcp,cpq->rcq", window, masked, preferred_element_type=jnp.float32
            )
    ladder = ladder.reshape(rows_dev, cols_dev)
    all_rows = lax.all_gather(cycle_input, "occ", axis=0, tiled=True)
    cycle_part = jnp.einsum(
        "ijba,jbkc->ikca", all_rows, cycle_integrals, preferred_element_type=jnp.float32
    ).astype(jnp.bfloat16)
    cycle_pair = lax.all_to_all(
        lax.all_to_all(cycle_part, "occ", split_axis=0, concat_axis=1, tiled=True),
        "vir",
        split_axis=2,
        concat_axis=3,
        tiled=True,
    )
    cycle_flat = cycle_pair.reshape(rows_dev, cols_dev)
    denominator = row_gap[:, None] + column_energy[None, :]
    updated = (
        amplitudes.astype(jnp.float32) + (cycle_flat.astype(jnp.float32) + ladder) / denominator
    )
    return updated.astype(jnp.bfloat16)


def solution(mesh):
    in_specs = (
        P("occ", "vir"),
        P(None, None, "occ", None),
        P("vir", None, None, None),
        P("vir", None),
        P("vir"),
        P("occ"),
        P("vir"),
    )
    out_specs = P("occ", "vir")
    return jax.shard_map(local, mesh=mesh, in_specs=in_specs, out_specs=out_specs, check_vma=False)
```

profile of v0, /device:TPU:1, one launch (start us, length us, event | category | flops | bytes accessed | tf_op | source)
XLA Modules:
  0.0 195.1 jit_solution(11123908715003614297)
XLA Ops:
  7.3 4.9 %collective-permute-start = (bf16[64,256]{1,0:T(8,128)(2,1)S(1)}, bf16[64,256]{1,0:T(8,128)(2,1)S(1)}, u32[]{:S(2)}, u32[]{:S(2)}) collective-permute-start(bf16[64,256]{1,0:T(8,128)(2,1)S(1)} %get-tuple-element.11), channel_id=1, source_target_pairs={{0,1},{1,2},{2,3},{3,4},{4,5},{5,6},{6,7},{7,8},{8,9},{9,10},{10,1... | collective-permute-start | bytes 98312 | tf_op jit(solution)/shard_map/ppermute | solution.py:19
  16.0 9.4 %copy.133 = bf16[4,16,2,4096]{1,0,2,3:T(4,128)(2,1)} copy(bf16[4,16,2,4096]{3,2,1,0:T(2,128)(2,1)S(1)} %reshape.294) | data formatting | bytes 2097152 | tf_op jit(solution)/shard_map/reshape | solution.py:33
  25.5 11.2 %reshape.306 = bf16[32,2,8192]{2,1,0:T(2,128)(2,1)} reshape(bf16[4096,2,4,16]{3,2,1,0:T(4,128)(2,1)} %bitcast.213) | data formatting | bytes 2097152
  36.7 8.4 %all-to-all-start = ((bf16[32,2,8192]{2,1,0:T(2,128)(2,1)}), bf16[32,2,8192]{2,1,0:T(2,128)(2,1)S(1)}, u32[]{:S(2)}, u32[]{:S(2)}) async-start(bf16[32,2,8192]{2,1,0:T(2,128)(2,1)} %reshape.306), calls=%async_computation | async-start | bytes 2097152 | tf_op jit(solution)/shard_map/all_to_all | solution.py:34
  45.3 3.7 %fusion.12 = f32[64,128,64]{1,2,0:T(8,128)} fusion(pred[64]{0:T(512)(128)(4,1)S(1)} %get-tuple-element.23, bf16[64,4,128,128]{3,2,1,0:T(8,128)(2,1)} %param.9, bf16[64,8192]{1,0:T(8,128)(2,1)S(1)} %copy-done), kind=kOutput, calls=%fused_computation.23 | convolution fusion | flops 135266304 | bytes 5242944 | tf_op jit(solution)/shard_map/rcp,cpq->rcq/dot_general | solution.py:50
  49.0 3.6 %fusion.17 = f32[64,128,64]{1,2,0:T(8,128)} fusion(pred[64]{0:T(512)(128)(4,1)S(1)} %get-tuple-element.15, bf16[64,4,128,128]{3,2,1,0:T(8,128)(2,1)} %param.9, bf16[64,8192]{1,0:T(8,128)(2,1)S(1)} %copy-done), kind=kOutput, calls=%fused_computation.33 | convolution fusion | flops 135266304 | bytes 5242944 | tf_op jit(solution)/shard_map/rcp,cpq->rcq/dot_general | solution.py:50
  52.7 3.7 %fusion.23 = f32[64,128,64]{1,2,0:T(8,128)} fusion(pred[64]{0:T(512)(128)(4,1)S(1)} %get-tuple-element.19, bf16[64,4,128,128]{3,2,1,0:T(8,128)(2,1)} %param.9, bf16[64,8192]{1,0:T(8,128)(2,1)S(1)} %copy-done), kind=kOutput, calls=%fused_computation.48 | convolution fusion | flops 135266304 | bytes 5242944 | tf_op jit(solution)/shard_map/rcp,cpq->rcq/dot_general | solution.py:50
  56.3 5.7 %all-to-all-done = bf16[32,2,8192]{2,1,0:T(2,128)(2,1)S(1)} async-done(((bf16[32,2,8192]{2,1,0:T(2,128)(2,1)}), bf16[32,2,8192]{2,1,0:T(2,128)(2,1)S(1)}, u32[]{:S(2)}, u32[]{:S(2)}) %all-to-all-start) | async-done | bytes 1048608 | tf_op jit(solution)/shard_map/all_to_all | solution.py:34
  62.0 7.6 %reshape.307 = bf16[4096,2,4,16]{3,2,1,0:T(4,128)(2,1)} reshape(bf16[32,2,8192]{2,1,0:T(2,128)(2,1)S(1)} %all-to-all-done) | data formatting | bytes 2097152
  69.6 12.8 %copy.134 = bf16[4,16,32,2,128]{4,3,2,1,0:T(2,128)(2,1)} copy(bf16[4,16,32,2,128]{1,0,3,4,2:T(4,128)(2,1)} %bitcast.214) | data formatting | bytes 2097152 | tf_op jit(solution)/shard_map/all_to_all | solution.py:34
  82.4 3.9 %fusion.7 = f32[64,128,64]{1,2,0:T(8,128)} fusion(pred[64]{0:T(512)(128)(4,1)S(1)} %get-tuple-element.27, bf16[64,4,128,128]{3,2,1,0:T(8,128)(2,1)} %param.9, bf16[64,8192]{1,0:T(8,128)(2,1)S(1)} %copy-done), kind=kOutput, calls=%fused_computation.13 | convolution fusion | flops 135266304 | bytes 5242944 | tf_op jit(solution)/shard_map/rcp,cpq->rcq/dot_general | solution.py:50
  87.2 2.2 %slice-done.1 = s8[4194304]{0:T(1024)(128)(4,1)S(1)} async-done(((s8[8388608]{0:T(1024)(128)(4,1)}), s8[4194304]{0:T(1024)(128)(4,1)S(1)}, s32[]{:S(2)}) %slice-start.1) | async-done | bytes 4194328
  114.5 13.9 %all-gather.2.cloned.1.call-done = bf16[16,16,64,128]{3,2,1,0:T(8,128)(2,1)} async-done(((bf16[4,16,64,128]{3,2,1,0:T(8,128)(2,1)}), bf16[16,16,64,128]{3,2,1,0:T(8,128)(2,1)}) %all-gather.2.cloned.1.call-update) | async-done | bytes 4194320 | tf_op jit(solution)/shard_map/all_gather | solution.py:54
  128.4 3.5 %fusion.48 = bf16[16,4,64,128]{3,2,0,1:T(8,128)(2,1)S(1)} fusion(bf16[16,16,64,128]{3,2,1,0:T(8,128)(2,1)} %all-gather.2.cloned.1.call-done, bf16[16,64,4,64,1]{3,2,1,0,4:T(4,128)(2,1)S(1)} %bitcast.221), kind=kOutput, calls=%fused_computation.72 | convolution fusion | flops 1074266112 | bytes 5767168 | tf_op jit(solution)/shard_map/ijba,jbkc->ikca/dot_general | solution.py:55
  132.9 3.7 %all-to-all-start.1 = ((bf16[16,4,64,128]{3,2,1,0:T(8,128)(2,1)}), bf16[16,4,64,128]{3,2,1,0:T(8,128)(2,1)S(1)}, u32[]{:S(2)}, u32[]{:S(2)}) async-start(bf16[16,4,64,128]{3,2,1,0:T(8,128)(2,1)} %copy.136), calls=%async_computation.1 | async-start | bytes 2097152 | tf_op jit(solution)/shard_map/all_to_all | solution.py:59
  136.6 4.0 %fusion.6 = f32[64,128,64]{1,2,0:T(8,128)} fusion(pred[64]{0:T(512)(128)(4,1)S(1)} %get-tuple-element.26, bf16[64,4,128,128]{3,2,1,0:T(8,128)(2,1)} %param.9, bf16[8,64,8,128]{3,2,1,0:T(8,128)(2,1)} %copy-done.2), kind=kOutput, calls=%fused_computation.12 | convolution fusion | flops 135266304 | bytes 5242944 | tf_op jit(solution)/shard_map/rcp,cpq->rcq/dot_general | solution.py:50
  140.7 3.6 %fusion.10 = f32[64,128,64]{1,2,0:T(8,128)} fusion(pred[64]{0:T(512)(128)(4,1)S(1)} %get-tuple-element.32, bf16[64,4,128,128]{3,2,1,0:T(8,128)(2,1)} %param.9, bf16[8,64,8,128]{3,2,1,0:T(8,128)(2,1)S(1)} %get-tuple-element.5), kind=kOutput, calls=%fused_computation.21 | convolution fusion | flops 135266304 | bytes 5242944 | tf_op jit(solution)/shard_map/rcp,cpq->rcq/dot_general | solution.py:50
  144.3 3.6 %fusion.15 = f32[64,128,64]{1,2,0:T(8,128)} fusion(pred[64]{0:T(512)(128)(4,1)S(1)} %get-tuple-element.31, bf16[64,4,128,128]{3,2,1,0:T(8,128)(2,1)} %param.9, bf16[8,64,8,128]{3,2,1,0:T(8,128)(2,1)S(1)} %get-tuple-element.5), kind=kOutput, calls=%fused_computation.31 | convolution fusion | flops 135266304 | bytes 5242944 | tf_op jit(solution)/shard_map/rcp,cpq->rcq/dot_general | solution.py:50
  147.9 2.9 %all-to-all-done.1 = bf16[16,4,64,128]{3,2,1,0:T(8,128)(2,1)S(1)} async-done(((bf16[16,4,64,128]{3,2,1,0:T(8,128)(2,1)}), bf16[16,4,64,128]{3,2,1,0:T(8,128)(2,1)S(1)}, u32[]{:S(2)}, u32[]{:S(2)}) %all-to-all-start.1) | async-done | bytes 1048608 | tf_op jit(solution)/shard_map/all_to_all | solution.py:59
  152.6 8.6 %all-to-all-start.2 = ((bf16[4,16,64,128]{3,1,0,2:T(8,128)(2,1)}), bf16[4,16,64,128]{3,1,0,2:T(8,128)(2,1)}, u32[]{:S(2)}, u32[]{:S(2)}) async-start(bf16[4,16,64,128]{3,1,0,2:T(8,128)(2,1)} %copy.138), calls=%async_computation.2 | async-start | bytes 2097152 | tf_op jit(solution)/shard_map/all_to_all | solution.py:58
  161.3 15.6 %fusion.20 = f32[64,8,8,128]{3,2,1,0:T(8,128)S(1)} fusion(f32[64,128,64]{1,2,0:T(8,128)} %fusion.9, f32[64,128,64]{1,2,0:T(8,128)} %fusion.14, f32[64,128,64]{1,2,0:T(8,128)} %fusion.19, f32[64,128,64]{1,2,0:T(8,128)} %fusion.8, f32[64,128,64]{1,2,0:T(8,128)} %fusion.13, f32[64,128,64]{1,2,0:T(8,128)} %fusion.24, f32[64,128,64]{1,2,0:T(8,128)} %fusion.18, ...), kind=kOutput, calls=%fused_computation.38 | convolution fusion | flops 145227776 | bytes 45088832 | tf_op jit(solution)/shard_map/rcp,cpq->rcq/dot_general | solution.py:50
  179.9 2.6 %copy.140 = f32[4,16,2,32,128]{4,3,2,1,0:T(8,128)} copy(f32[4,16,2,32,128]{4,1,2,3,0:T(8,128)S(1)} %convert_bitcast_fusion) | data formatting | bytes 4194304 | tf_op jit(solution)/shard_map/convert_element_type | solution.py:68
  182.5 2.7 %reshape.301 = f32[64,8192]{1,0:T(8,128)} reshape(f32[4,16,2,32,128]{4,3,2,1,0:T(8,128)} %copy.140) | data formatting | bytes 4194304 | tf_op jit(solution)/shard_map/convert_element_type | solution.py:68
  185.2 3.1 %fusion.4 = bf16[64,8192]{1,0:T(8,128)(2,1)} fusion(f32[64,8192]{1,0:T(8,128)} %reshape.301, f32[64,8,8,128]{3,2,1,0:T(8,128)S(1)} %fusion.20, bf16[64,8192]{1,0:T(8,128)(2,1)S(1)} %copy-done, f32[8192]{0:T(1024)S(1)} %copy-done.3, f32[64]{0:T(128)S(1)} %copy-done.5), kind=kLoop, calls=%fused_computation.5 | loop fusion | flops 3145728 | bytes 6324480 | tf_op jit(solution)/shard_map/convert_element_type | solution.py:70
  (56 shorter events, 36.4 us)
Async XLA Ops:
  7.3 79.0 %collective-permute-start = (bf16[64,256]{1,0:T(8,128)(2,1)S(1)}, bf16[64,256]{1,0:T(8,128)(2,1)S(1)}, u32[]{:S(2)}, u32[]{:S(2)}) collective-permute-start(bf16[64,256]{1,0:T(8,128)(2,1)S(1)} %get-tuple-element.11), channel_id=1, source_target_pairs={{0,1},{1,2},{2,3},{3,4},{4,5},{5,6},{6,7},{7,8},{8,9},{9,10},{10,1... | collective-permute-start | bytes 98312 | tf_op jit(solution)/shard_map/ppermute | solution.py:19
  12.2 74.3 %collective-permute-start.1 = (bf16[64,256]{1,0:T(8,128)(2,1)S(1)}, bf16[64,256]{1,0:T(8,128)(2,1)S(1)}, u32[]{:S(2)}, u32[]{:S(2)}) collective-permute-start(bf16[64,256]{1,0:T(8,128)(2,1)S(1)} %get-tuple-element.12), channel_id=1, source_target_pairs={{1,0},{2,1},{3,2},{4,3},{5,4},{6,5},{7,6},{8,7},{9,8},{10,9},{11,1... | collective-permute-start | bytes 98312 | tf_op jit(solution)/shard_map/ppermute | solution.py:22
  36.7 8.5 %copy-start.7 = (s32[64]{0:T(128)S(1)}, s32[64]{0:T(128)}, u32[]{:S(2)}) copy-start(s32[64]{0:T(128)} %param.11) | copy-start | bytes 772
  36.7 8.5 %copy-start.4 = (s32[64,4]{0,1:T(4,128)S(1)}, s32[64,4]{0,1:T(4,128)}, u32[]{:S(2)}) copy-start(s32[64,4]{0,1:T(4,128)} %param.10) | copy-start | bytes 3076
  36.7 8.6 %copy-start = (bf16[64,8192]{1,0:T(8,128)(2,1)S(1)}, bf16[64,8192]{1,0:T(8,128)(2,1)}, u32[]{:S(2)}) copy-start(bf16[64,8192]{1,0:T(8,128)(2,1)} %param.7) | copy-start | bytes 3145732
  36.7 25.4 %all-to-all-start = ((bf16[32,2,8192]{2,1,0:T(2,128)(2,1)}), bf16[32,2,8192]{2,1,0:T(2,128)(2,1)S(1)}, u32[]{:S(2)}, u32[]{:S(2)}) async-start(bf16[32,2,8192]{2,1,0:T(2,128)(2,1)} %reshape.306), calls=%async_computation | async-start | bytes 2097152 | tf_op jit(solution)/shard_map/all_to_all | solution.py:34
  45.1 83.3 %all-gather.2.cloned.1.call-start = ((), (), s32[]{:S(2)}) async-start(), calls=%async_computation.3 | async-start | bytes 5242880 | tf_op jit(solution)/shard_map/all_gather | solution.py:54
  82.4 4.8 %slice-start = ((s8[8388608]{0:T(1024)(128)(4,1)}), s8[4194304]{0:T(1024)(128)(4,1)S(1)}, s32[]{:S(2)}) async-start(s8[8388608]{0:T(1024)(128)(4,1)} %bitcast.219), calls=%async_computation.4 | async-start | bytes 8388608
  86.3 3.1 %slice-start.1 = ((s8[8388608]{0:T(1024)(128)(4,1)}), s8[4194304]{0:T(1024)(128)(4,1)S(1)}, s32[]{:S(2)}) async-start(s8[8388608]{0:T(1024)(128)(4,1)} %bitcast.219), calls=%async_computation.5 | async-start | bytes 8388608
  86.9 15.1 %copy-start.1 = (bf16[8,64,8,128]{3,2,1,0:T(8,128)(2,1)}, bf16[8,64,8,128]{3,2,1,0:T(8,128)(2,1)S(1)}, u32[]{:S(2)}) copy-start(bf16[8,64,8,128]{3,2,1,0:T(8,128)(2,1)S(1)} %get-tuple-element.8) | copy-start | bytes 3145732
  87.2 21.1 %copy-start.2 = (bf16[8,64,8,128]{3,2,1,0:T(8,128)(2,1)}, bf16[8,64,8,128]{3,2,1,0:T(8,128)(2,1)S(1)}, u32[]{:S(2)}) copy-start(bf16[8,64,8,128]{3,2,1,0:T(8,128)(2,1)S(1)} %get-tuple-element.6) | copy-start | bytes 3145732
  112.5 15.9 %copy-start.6 = (bf16[16,64,4,64]{3,2,1,0:T(4,128)(2,1)S(1)}, bf16[16,64,4,64]{3,2,1,0:T(4,128)(2,1)}, u32[]{:S(2)}) copy-start(bf16[16,64,4,64]{3,2,1,0:T(4,128)(2,1)} %param.8) | copy-start | bytes 1572868
  132.9 18.0 %all-to-all-start.1 = ((bf16[16,4,64,128]{3,2,1,0:T(8,128)(2,1)}), bf16[16,4,64,128]{3,2,1,0:T(8,128)(2,1)S(1)}, u32[]{:S(2)}, u32[]{:S(2)}) async-start(bf16[16,4,64,128]{3,2,1,0:T(8,128)(2,1)} %copy.136), calls=%async_computation.1 | async-start | bytes 2097152 | tf_op jit(solution)/shard_map/all_to_all | solution.py:59
  152.6 25.6 %all-to-all-start.2 = ((bf16[4,16,64,128]{3,1,0,2:T(8,128)(2,1)}), bf16[4,16,64,128]{3,1,0,2:T(8,128)(2,1)}, u32[]{:S(2)}, u32[]{:S(2)}) async-start(bf16[4,16,64,128]{3,1,0,2:T(8,128)(2,1)} %copy.138), calls=%async_computation.2 | async-start | bytes 2097152 | tf_op jit(solution)/shard_map/all_to_all | solution.py:58
  182.5 2.7 %copy-start.3 = (f32[8192]{0:T(1024)S(1)}, f32[8192]{0:T(1024)}, u32[]{:S(2)}) copy-start(f32[8192]{0:T(1024)} %param.13) | copy-start | bytes 98308
  182.5 2.7 %copy-start.5 = (f32[64]{0:T(128)S(1)}, f32[64]{0:T(128)}, u32[]{:S(2)}) copy-start(f32[64]{0:T(128)} %param.12) | copy-start | bytes 772
Sparse Core Ops, SparseCore 0:
  82.6 45.7 all-gather.1
where the time goes:
time: 196 us; the launch traced here: 195 us
  matrix products  70.3 us (36%)
  local copies, waits for them, and re-layouts  56.1 us (29%)
  starting transfers between devices  27.7 us (14%)
  waiting for transfers between devices  23.9 us (12%)
  between operations  13.7 us (7%)
  other arithmetic  3.39 us (2%)
    dot_general x20, matrix products, local(): jnp.einsum('rcp,cpq->rcq', window, masked, preferred_element_type=jnp.flo...  66.9 us
    unnamed x25, local copies, waits for them, and re-layouts  21.7 us
    all_gather x1, waiting for transfers between devices, local(): all_rows = lax.all_gather(cycle_input, 'occ', axis=0, tiled=True)  13.9 us
    all_to_all x1, local copies, waits for them, and re-layouts, local(): lax.all_to_all(four_dim, 'vir', split_axis=3, concat_axis=2, tiled=True)  12.8 us
    reshape x2, local copies, waits for them, and re-layouts, local(): four_dim = amplitudes.reshape(outer_occ, NJ, NB_DEV, NA)  11.3 us
    all_to_all x1, starting transfers between devices, local(): lax.all_to_all(lax.all_to_all(cycle_part, 'occ', split_axis=0, concat_axi...  8.64 us
    all_to_all x1, starting transfers between devices, local(): lax.all_to_all(four_dim, 'vir', split_axis=3, concat_axis=2, tiled=True)  8.45 us
    all_to_all x1, waiting for transfers between devices, local(): lax.all_to_all(four_dim, 'vir', split_axis=3, concat_axis=2, tiled=True)  5.69 us
  transfers between devices with their start and end apart: 6, of which 4 were waited for; matrix products, arithmetic and copies ran while one was open for 57% of the time, Pallas kernels for 0%

commit v1 on v0

--- a/solution.py
+++ b/solution.py
@@ -2,6 +2,7 @@
 import jax.numpy as jnp
 from jax import lax
 from jax.sharding import PartitionSpec as P
+from jax.lax import all_to_all, axis_size
 
 TILE = 128
 NJ = 16
@@ -31,7 +32,10 @@
     cols_dev = amplitudes.shape[1]
     outer_occ = rows_dev // NJ
     four_dim = amplitudes.reshape(outer_occ, NJ, NB_DEV, NA)
-    cycle_input = lax.all_to_all(four_dim, "vir", split_axis=3, concat_axis=2, tiled=True)
+    cycle_input = jnp.concatenate(
+        all_to_all(jnp.stack(jnp.split(four_dim, axis_size("vir"), axis=3), axis=0), "vir", 0, 0),
+        axis=2,
+    )
     tiles_dev = cols_dev // TILE
     padded = extended(amplitudes, (("vir", 1),), HT * TILE)
     own_tiles = lax.axis_index("vir") * tiles_dev + jnp.arange(tiles_dev, dtype=jnp.int32)

time: 196 us -> 177 us (0.903)
  local copies, waits for them, and re-layouts: 56.1 us -> 35.3 us
  matrix products: 70.3 us -> 74.8 us
  waiting for transfers between devices: 23.9 us -> 21.5 us
    all_to_all x1, local copies, waits for them, and re-layouts: 12.8 us -> 0.2 us  [local(): all_to_all(jnp.stack(jnp.split(four_dim, axis_size('vir'), axis=3), axis=...]
    reshape x2 -> x1, local copies, waits for them, and re-layouts: 11.3 us -> 1.83 us  [local(): four_dim = amplitudes.reshape(outer_occ, NJ, NB_DEV, NA)]
    dot_general x20, matrix products: 66.9 us -> 70.3 us  [local(): jnp.einsum('rcp,cpq->rcq', window, masked, preferred_element_type=jnp.flo...]
    all_gather x1, waiting for transfers between devices: 13.9 us -> 11.5 us  [local(): all_rows = lax.all_gather(cycle_input, 'occ', axis=0, tiled=True)]
    unnamed x25 -> x61, local copies, waits for them, and re-layouts: 21.7 us -> 21.9 us
  transfers between devices with their start and end apart: 6 -> 6, of which waited for: 4 -> 4; matrix products, arithmetic and copies ran while one was open for 57% -> 55% of each run, Pallas kernels for 0% -> 0%
where the time goes in v1:
time: 177 us; the launch traced here: 176 us
  matrix products  74.8 us (42%)
  local copies, waits for them, and re-layouts  35.3 us (20%)
  starting transfers between devices  27.7 us (16%)
  waiting for transfers between devices  21.5 us (12%)
  between operations  13.7 us (8%)
  other arithmetic  3.39 us (2%)
    dot_general x20, matrix products, local(): jnp.einsum('rcp,cpq->rcq', window, masked, preferred_element_type=jnp.flo...  70.3 us
    unnamed x61, local copies, waits for them, and re-layouts  21.9 us
    all_gather x1, waiting for transfers between devices, local(): all_rows = lax.all_gather(cycle_input, 'occ', axis=0, tiled=True)  11.5 us
    all_to_all x1, starting transfers between devices, local(): lax.all_to_all(lax.all_to_all(cycle_part, 'occ', split_axis=0, concat_axi...  8.63 us
    all_to_all x1, starting transfers between devices, local(): all_to_all(jnp.stack(jnp.split(four_dim, axis_size('vir'), axis=3), axis=...  8.31 us
    all_to_all x1, waiting for transfers between devices, local(): all_to_all(jnp.stack(jnp.split(four_dim, axis_size('vir'), axis=3), axis=...  5.57 us
    convert_element_type x2, local copies, waits for them, and re-layouts, local(): cycle_flat.astype(jnp.float32) + ladder  5.33 us
    ppermute x1, starting transfers between devices, extended(): lax.ppermute(lax.slice_in_dim(block, block.shape[dim] - width, None, axis...  4.92 us
  transfers between devices with their start and end apart: 6, of which 4 were waited for; matrix products, arithmetic and copies ran while one was open for 55% of the time, Pallas kernels for 0%

profile of v1, /device:TPU:1, one launch (start us, length us, event | category | flops | bytes accessed | tf_op | source)
XLA Modules:
  0.0 176.4 jit_solution(17974415051826759850)
XLA Ops:
  7.3 4.9 %collective-permute-start = (bf16[64,256]{1,0:T(8,128)(2,1)S(1)}, bf16[64,256]{1,0:T(8,128)(2,1)S(1)}, u32[]{:S(2)}, u32[]{:S(2)}) collective-permute-start(bf16[64,256]{1,0:T(8,128)(2,1)S(1)} %get-tuple-element.11), channel_id=1, source_target_pairs={{0,1},{1,2},{2,3},{3,4},{4,5},{5,6},{6,7},{7,8},{8,9},{9,10},{10,1... | collective-permute-start | bytes 98312 | tf_op jit(solution)/shard_map/ppermute | solution.py:20
  36.9 8.3 %all-to-all-start = ((bf16[32,4,16,2,128]{4,3,2,1,0:T(2,128)(2,1)}), bf16[32,4,16,2,128]{4,3,2,1,0:T(2,128)(2,1)S(1)}, u32[]{:S(2)}, u32[]{:S(2)}) async-start(bf16[32,4,16,2,128]{4,3,2,1,0:T(2,128)(2,1)} %constant_dynamic-update-slice_fusion), calls=%async_computation | async-start | bytes 2097152 | tf_op jit(solution)/shard_map/all_to_all | solution.py:36
  45.4 3.7 %fusion.12 = f32[64,128,64]{1,2,0:T(8,128)} fusion(pred[64]{0:T(512)(128)(4,1)S(1)} %get-tuple-element.23, bf16[64,4,128,128]{3,2,1,0:T(8,128)(2,1)} %param.9, bf16[64,8192]{1,0:T(8,128)(2,1)S(1)} %copy-done), kind=kOutput, calls=%fused_computation.23 | convolution fusion | flops 135266304 | bytes 5242944 | tf_op jit(solution)/shard_map/rcp,cpq->rcq/dot_general | solution.py:54
  49.1 3.7 %fusion.17 = f32[64,128,64]{1,2,0:T(8,128)} fusion(pred[64]{0:T(512)(128)(4,1)S(1)} %get-tuple-element.15, bf16[64,4,128,128]{3,2,1,0:T(8,128)(2,1)} %param.9, bf16[64,8192]{1,0:T(8,128)(2,1)S(1)} %copy-done), kind=kOutput, calls=%fused_computation.33 | convolution fusion | flops 135266304 | bytes 5242944 | tf_op jit(solution)/shard_map/rcp,cpq->rcq/dot_general | solution.py:54
  52.8 3.7 %fusion.23 = f32[64,128,64]{1,2,0:T(8,128)} fusion(pred[64]{0:T(512)(128)(4,1)S(1)} %get-tuple-element.19, bf16[64,4,128,128]{3,2,1,0:T(8,128)(2,1)} %param.9, bf16[64,8192]{1,0:T(8,128)(2,1)S(1)} %copy-done), kind=kOutput, calls=%fused_computation.48 | convolution fusion | flops 135266304 | bytes 5242944 | tf_op jit(solution)/shard_map/rcp,cpq->rcq/dot_general | solution.py:54
  56.5 5.6 %all-to-all-done = bf16[32,4,16,2,128]{4,3,2,1,0:T(2,128)(2,1)S(1)} async-done(((bf16[32,4,16,2,128]{4,3,2,1,0:T(2,128)(2,1)}), bf16[32,4,16,2,128]{4,3,2,1,0:T(2,128)(2,1)S(1)}, u32[]{:S(2)}, u32[]{:S(2)}) %all-to-all-start) | async-done | bytes 1048608 | tf_op jit(solution)/shard_map/all_to_all | solution.py:36
  63.6 3.8 %fusion.7 = f32[64,128,64]{1,2,0:T(8,128)} fusion(pred[64]{0:T(512)(128)(4,1)S(1)} %get-tuple-element.27, bf16[64,4,128,128]{3,2,1,0:T(8,128)(2,1)} %param.9, bf16[64,8192]{1,0:T(8,128)(2,1)S(1)} %copy-done), kind=kOutput, calls=%fused_computation.13 | convolution fusion | flops 135266304 | bytes 5242944 | tf_op jit(solution)/shard_map/rcp,cpq->rcq/dot_general | solution.py:54
  69.4 5.7 %fusion.13 = f32[64,128,64]{1,2,0:T(8,128)} fusion(pred[64]{0:T(512)(128)(4,1)S(1)} %get-tuple-element.24, bf16[64,4,128,128]{3,2,1,0:T(8,128)(2,1)} %param.9, bf16[8,64,8,128]{3,2,1,0:T(8,128)(2,1)S(1)} %get-tuple-element.7), kind=kOutput, calls=%fused_computation.24 | convolution fusion | flops 135266304 | bytes 5242944 | tf_op jit(solution)/shard_map/rcp,cpq->rcq/dot_general | solution.py:54
  75.1 2.1 %fusion.18 = f32[64,128,64]{1,2,0:T(8,128)} fusion(pred[64]{0:T(512)(128)(4,1)S(1)} %get-tuple-element.16, bf16[64,4,128,128]{3,2,1,0:T(8,128)(2,1)S(1)} %bitcast.347, bf16[8,64,8,128]{3,2,1,0:T(8,128)(2,1)S(1)} %get-tuple-element.7), kind=kOutput, calls=%fused_computation.34 | convolution fusion | flops 135266304 | bytes 5243392 | tf_op jit(solution)/shard_map/rcp,cpq->rcq/dot_general | solution.py:54
  81.4 2.1 %fusion.24 = f32[64,128,64]{1,2,0:T(8,128)} fusion(pred[64]{0:T(512)(128)(4,1)S(1)} %get-tuple-element.20, bf16[64,4,128,128]{3,2,1,0:T(8,128)(2,1)S(1)} %bitcast.347, bf16[8,64,8,128]{3,2,1,0:T(8,128)(2,1)S(1)} %get-tuple-element.7), kind=kOutput, calls=%fused_computation.49 | convolution fusion | flops 135266304 | bytes 5243392 | tf_op jit(solution)/shard_map/rcp,cpq->rcq/dot_general | solution.py:54
  87.7 2.1 %fusion.11 = f32[64,128,64]{1,2,0:T(8,128)} fusion(pred[64]{0:T(512)(128)(4,1)S(1)} %get-tuple-element.21, bf16[64,4,128,128]{3,2,1,0:T(8,128)(2,1)S(1)} %bitcast.347, bf16[8,64,8,128]{3,2,1,0:T(8,128)(2,1)S(1)} %get-tuple-element.6), kind=kOutput, calls=%fused_computation.22 | convolution fusion | flops 135266304 | bytes 5243392 | tf_op jit(solution)/shard_map/rcp,cpq->rcq/dot_general | solution.py:54
  93.9 2.1 %fusion.21 = f32[64,128,64]{1,2,0:T(8,128)} fusion(pred[64]{0:T(512)(128)(4,1)S(1)} %get-tuple-element.22, bf16[64,4,128,128]{3,2,1,0:T(8,128)(2,1)S(1)} %bitcast.347, bf16[8,64,8,128]{3,2,1,0:T(8,128)(2,1)S(1)} %get-tuple-element.5), kind=kOutput, calls=%fused_computation.46 | convolution fusion | flops 135266304 | bytes 5243392 | tf_op jit(solution)/shard_map/rcp,cpq->rcq/dot_general | solution.py:54
  98.1 11.5 %all-gather.2.cloned.1.call-done = bf16[16,16,64,128]{3,2,1,0:T(8,128)(2,1)} async-done(((bf16[4,16,64,128]{3,2,1,0:T(8,128)(2,1)}), bf16[16,16,64,128]{3,2,1,0:T(8,128)(2,1)}) %all-gather.2.cloned.1.call-update) | async-done | bytes 4194320 | tf_op jit(solution)/shard_map/all_gather | solution.py:58
  109.5 4.5 %fusion.48 = bf16[16,4,64,128]{3,2,1,0:T(8,128)(2,1)} fusion(bf16[16,16,64,128]{3,2,1,0:T(8,128)(2,1)} %all-gather.2.cloned.1.call-done, bf16[16,64,4,64]{1,3,0,2:T(8,128)(2,1)S(1)} %copy.195), kind=kOutput, calls=%fused_computation.72 | convolution fusion | flops 1074266112 | bytes 5767168 | tf_op jit(solution)/shard_map/ijba,jbkc->ikca/dot_general | solution.py:59
  114.0 3.9 %all-to-all-start.1 = ((bf16[16,4,64,128]{3,2,1,0:T(8,128)(2,1)}), bf16[16,4,64,128]{3,2,1,0:T(8,128)(2,1)S(1)}, u32[]{:S(2)}, u32[]{:S(2)}) async-start(bf16[16,4,64,128]{3,2,1,0:T(8,128)(2,1)} %fusion.48), calls=%async_computation.1 | async-start | bytes 2097152 | tf_op jit(solution)/shard_map/all_to_all | solution.py:63
  117.9 3.8 %fusion.6 = f32[64,128,64]{1,2,0:T(8,128)} fusion(pred[64]{0:T(512)(128)(4,1)S(1)} %get-tuple-element.26, bf16[64,4,128,128]{3,2,1,0:T(8,128)(2,1)} %param.9, bf16[8,64,8,128]{3,2,1,0:T(8,128)(2,1)S(1)} %copy-done.6), kind=kOutput, calls=%fused_computation.12 | convolution fusion | flops 135266304 | bytes 5242944 | tf_op jit(solution)/shard_map/rcp,cpq->rcq/dot_general | solution.py:54
  121.7 3.7 %fusion.10 = f32[64,128,64]{1,2,0:T(8,128)} fusion(pred[64]{0:T(512)(128)(4,1)S(1)} %get-tuple-element.32, bf16[64,4,128,128]{3,2,1,0:T(8,128)(2,1)} %param.9, bf16[8,64,8,128]{3,2,1,0:T(8,128)(2,1)S(1)} %copy-done.4), kind=kOutput, calls=%fused_computation.21 | convolution fusion | flops 135266304 | bytes 5242944 | tf_op jit(solution)/shard_map/rcp,cpq->rcq/dot_general | solution.py:54
  125.4 3.6 %fusion.15 = f32[64,128,64]{1,2,0:T(8,128)} fusion(pred[64]{0:T(512)(128)(4,1)S(1)} %get-tuple-element.31, bf16[64,4,128,128]{3,2,1,0:T(8,128)(2,1)} %param.9, bf16[8,64,8,128]{3,2,1,0:T(8,128)(2,1)S(1)} %copy-done.4), kind=kOutput, calls=%fused_computation.31 | convolution fusion | flops 135266304 | bytes 5242944 | tf_op jit(solution)/shard_map/rcp,cpq->rcq/dot_general | solution.py:54
  129.0 3.1 %all-to-all-done.1 = bf16[16,4,64,128]{3,2,1,0:T(8,128)(2,1)S(1)} async-done(((bf16[16,4,64,128]{3,2,1,0:T(8,128)(2,1)}), bf16[16,4,64,128]{3,2,1,0:T(8,128)(2,1)S(1)}, u32[]{:S(2)}, u32[]{:S(2)}) %all-to-all-start.1) | async-done | bytes 1048608 | tf_op jit(solution)/shard_map/all_to_all | solution.py:63
  133.9 8.6 %all-to-all-start.2 = ((bf16[4,16,64,128]{3,1,0,2:T(8,128)(2,1)}), bf16[4,16,64,128]{3,1,0,2:T(8,128)(2,1)}, u32[]{:S(2)}, u32[]{:S(2)}) async-start(bf16[4,16,64,128]{3,1,0,2:T(8,128)(2,1)} %copy.197), calls=%async_computation.2 | async-start | bytes 2097152 | tf_op jit(solution)/shard_map/all_to_all | solution.py:62
  142.5 15.6 %fusion.20 = f32[64,8,8,128]{3,2,1,0:T(8,128)S(1)} fusion(f32[64,128,64]{1,2,0:T(8,128)} %fusion.9, f32[64,128,64]{1,2,0:T(8,128)} %fusion.14, f32[64,128,64]{1,2,0:T(8,128)} %fusion.19, f32[64,128,64]{1,2,0:T(8,128)} %fusion.8, f32[64,128,64]{1,2,0:T(8,128)} %fusion.13, f32[64,128,64]{1,2,0:T(8,128)} %fusion.24, f32[64,128,64]{1,2,0:T(8,128)} %fusion.18, ...), kind=kOutput, calls=%fused_computation.38 | convolution fusion | flops 145227776 | bytes 45088832 | tf_op jit(solution)/shard_map/rcp,cpq->rcq/dot_general | solution.py:54
  161.2 2.6 %copy.199 = f32[4,16,2,32,128]{4,3,2,1,0:T(8,128)} copy(f32[4,16,2,32,128]{4,1,2,3,0:T(8,128)S(1)} %convert_bitcast_fusion) | data formatting | bytes 4194304 | tf_op jit(solution)/shard_map/convert_element_type | solution.py:72
  163.7 2.7 %reshape.309 = f32[64,8192]{1,0:T(8,128)} reshape(f32[4,16,2,32,128]{4,3,2,1,0:T(8,128)} %copy.199) | data formatting | bytes 4194304 | tf_op jit(solution)/shard_map/convert_element_type | solution.py:72
  166.5 3.1 %fusion.4 = bf16[64,8192]{1,0:T(8,128)(2,1)} fusion(f32[64,8192]{1,0:T(8,128)} %reshape.309, f32[64,8,8,128]{3,2,1,0:T(8,128)S(1)} %fusion.20, bf16[64,8192]{1,0:T(8,128)(2,1)S(1)} %copy-done, f32[8192]{0:T(1024)S(1)} %copy-done.7, f32[64]{0:T(128)S(1)} %copy-done.9), kind=kLoop, calls=%fused_computation.5 | loop fusion | flops 3145728 | bytes 6324480 | tf_op jit(solution)/shard_map/convert_element_type | solution.py:74
  (92 shorter events, 48.1 us)
Async XLA Ops:
  7.3 61.1 %collective-permute-start = (bf16[64,256]{1,0:T(8,128)(2,1)S(1)}, bf16[64,256]{1,0:T(8,128)(2,1)S(1)}, u32[]{:S(2)}, u32[]{:S(2)}) collective-permute-start(bf16[64,256]{1,0:T(8,128)(2,1)S(1)} %get-tuple-element.11), channel_id=1, source_target_pairs={{0,1},{1,2},{2,3},{3,4},{4,5},{5,6},{6,7},{7,8},{8,9},{9,10},{10,1... | collective-permute-start | bytes 98312 | tf_op jit(solution)/shard_map/ppermute | solution.py:20
  12.2 56.3 %collective-permute-start.1 = (bf16[64,256]{1,0:T(8,128)(2,1)S(1)}, bf16[64,256]{1,0:T(8,128)(2,1)S(1)}, u32[]{:S(2)}, u32[]{:S(2)}) collective-permute-start(bf16[64,256]{1,0:T(8,128)(2,1)S(1)} %get-tuple-element.12), channel_id=1, source_target_pairs={{1,0},{2,1},{3,2},{4,3},{5,4},{6,5},{7,6},{8,7},{9,8},{10,9},{11,1... | collective-permute-start | bytes 98312 | tf_op jit(solution)/shard_map/ppermute | solution.py:23
  16.0 29.2 %copy-start.10 = (s32[64]{0:T(128)S(1)}, s32[64]{0:T(128)}, u32[]{:S(2)}) copy-start(s32[64]{0:T(128)} %param.11) | copy-start | bytes 772
  16.0 29.3 %copy-start.8 = (s32[64,4]{0,1:T(4,128)S(1)}, s32[64,4]{0,1:T(4,128)}, u32[]{:S(2)}) copy-start(s32[64,4]{0,1:T(4,128)} %param.10) | copy-start | bytes 3076
  16.7 28.7 %copy-start = (bf16[64,8192]{1,0:T(8,128)(2,1)S(1)}, bf16[64,8192]{1,0:T(8,128)(2,1)}, u32[]{:S(2)}) copy-start(bf16[64,8192]{1,0:T(8,128)(2,1)} %param.7) | copy-start | bytes 3145732
  36.9 25.2 %all-to-all-start = ((bf16[32,4,16,2,128]{4,3,2,1,0:T(2,128)(2,1)}), bf16[32,4,16,2,128]{4,3,2,1,0:T(2,128)(2,1)S(1)}, u32[]{:S(2)}, u32[]{:S(2)}) async-start(bf16[32,4,16,2,128]{4,3,2,1,0:T(2,128)(2,1)} %constant_dynamic-update-slice_fusion), calls=%async_computation | async-start | bytes 2097152 | tf_op jit(solution)/shard_map/all_to_all | solution.py:36
  45.2 64.3 %all-gather.2.cloned.1.call-start = ((), (), s32[]{:S(2)}) async-start(), calls=%async_computation.3 | async-start | bytes 5242880 | tf_op jit(solution)/shard_map/all_gather | solution.py:58
  63.6 3.8 %copy-start.2 = (bf16[16,64,4,64]{3,2,1,0:T(4,128)(2,1)S(1)}, bf16[16,64,4,64]{3,2,1,0:T(4,128)(2,1)}, u32[]{:S(2)}) copy-start(bf16[16,64,4,64]{3,2,1,0:T(4,128)(2,1)} %param.8) | copy-start | bytes 1572868
  68.4 6.7 %slice-start = ((s8[8388608]{0:T(1024)(128)(4,1)}), s8[4194304]{0:T(1024)(128)(4,1)S(1)}, s32[]{:S(2)}) async-start(s8[8388608]{0:T(1024)(128)(4,1)} %bitcast.346), calls=%async_computation.4 | async-start | bytes 8388608
  69.0 16.6 %copy-start.1 = (bf16[8,64,8,128]{3,2,1,0:T(8,128)(2,1)}, bf16[8,64,8,128]{3,2,1,0:T(8,128)(2,1)S(1)}, u32[]{:S(2)}) copy-start(bf16[8,64,8,128]{3,2,1,0:T(8,128)(2,1)S(1)} %get-tuple-element.8) | copy-start | bytes 3145732
  69.0 6.1 %slice-start.1 = ((s8[8388608]{0:T(1024)(128)(4,1)}), s8[4194304]{0:T(1024)(128)(4,1)S(1)}, s32[]{:S(2)}) async-start(s8[8388608]{0:T(1024)(128)(4,1)} %bitcast.346), calls=%async_computation.5 | async-start | bytes 8388608
  69.4 22.5 %copy-start.5 = (bf16[8,64,8,128]{3,2,1,0:T(8,128)(2,1)}, bf16[8,64,8,128]{3,2,1,0:T(8,128)(2,1)S(1)}, u32[]{:S(2)}) copy-start(bf16[8,64,8,128]{3,2,1,0:T(8,128)(2,1)S(1)} %get-tuple-element.6) | copy-start | bytes 3145732
  69.4 26.6 %copy-start.3 = (bf16[8,64,8,128]{3,2,1,0:T(8,128)(2,1)}, bf16[8,64,8,128]{3,2,1,0:T(8,128)(2,1)S(1)}, u32[]{:S(2)}) copy-start(bf16[8,64,8,128]{3,2,1,0:T(8,128)(2,1)S(1)} %get-tuple-element.5) | copy-start | bytes 3145732
  114.0 3.9 %copy-start.6 = (bf16[8,64,8,128]{3,2,1,0:T(8,128)(2,1)S(1)}, bf16[8,64,8,128]{3,2,1,0:T(8,128)(2,1)}, u32[]{:S(2)}) copy-start(bf16[8,64,8,128]{3,2,1,0:T(8,128)(2,1)} %copy-done.5) | copy-start | bytes 3145732
  114.0 18.1 %all-to-all-start.1 = ((bf16[16,4,64,128]{3,2,1,0:T(8,128)(2,1)}), bf16[16,4,64,128]{3,2,1,0:T(8,128)(2,1)S(1)}, u32[]{:S(2)}, u32[]{:S(2)}) async-start(bf16[16,4,64,128]{3,2,1,0:T(8,128)(2,1)} %fusion.48), calls=%async_computation.1 | async-start | bytes 2097152 | tf_op jit(solution)/shard_map/all_to_all | solution.py:63
  117.9 3.8 %copy-start.4 = (bf16[8,64,8,128]{3,2,1,0:T(8,128)(2,1)S(1)}, bf16[8,64,8,128]{3,2,1,0:T(8,128)(2,1)}, u32[]{:S(2)}) copy-start(bf16[8,64,8,128]{3,2,1,0:T(8,128)(2,1)} %copy-done.3) | copy-start | bytes 3145732
  133.9 25.6 %all-to-all-start.2 = ((bf16[4,16,64,128]{3,1,0,2:T(8,128)(2,1)}), bf16[4,16,64,128]{3,1,0,2:T(8,128)(2,1)}, u32[]{:S(2)}, u32[]{:S(2)}) async-start(bf16[4,16,64,128]{3,1,0,2:T(8,128)(2,1)} %copy.197), calls=%async_computation.2 | async-start | bytes 2097152 | tf_op jit(solution)/shard_map/all_to_all | solution.py:62
  163.7 2.8 %copy-start.7 = (f32[8192]{0:T(1024)S(1)}, f32[8192]{0:T(1024)}, u32[]{:S(2)}) copy-start(f32[8192]{0:T(1024)} %param.13) | copy-start | bytes 98308
  163.7 2.8 %copy-start.9 = (f32[64]{0:T(128)S(1)}, f32[64]{0:T(128)}, u32[]{:S(2)}) copy-start(f32[64]{0:T(128)} %param.12) | copy-start | bytes 772
Sparse Core Ops, SparseCore 0:
  63.7 45.7 all-gather.1
